TPU v7x, 256 devices: a whole 4x4x8 slice. The times are simulated.
256 devices in a mesh: ctx: 64 (over x, z, core), head: 4 (over y).
Axes of the slice: x: 4, y: 4, z: 8, core: 2. Of those that a mesh axis runs over, the one named last changes fastest.
Arguments:
- queries: bfloat16 [8192, 8192], P('ctx', 'head'), may hold values from -7 to 7
- span_kv: bfloat16 [8192, 8, 256], P('ctx', 'head'), may hold values from -7 to 7
- cache_kv: bfloat16 [262144, 8, 256], P('ctx', 'head'), may hold values from -6 to 6
- verticals: int32 [8, 64], P('head'), may hold values from 0 to 4095, as said below
- offsets: int32 [8, 8], P('head'), may hold values from 0 to 7, as said below
Outputs:
- attended: bfloat16 [8192, 8192], P(('ctx', 'head'))
Inputs may be any that keep to these rules, and one draw needn't show every extreme that they name: `verticals`: each row holds 64 distinct cache blocks. Cache block b lies in the cache of index b // 64 of ctx; at most 2 blocks of one row lie in one index's cache, and in every row some index holds exactly 2. Each row holds 8 distinct offsets, 0 among them; some row holds 7.
All inputs are finite; a program needn't handle non-finite values.
Results may differ from a plain program's by a relative error of at most 0.0065.
Values may be sent and summed in bfloat16 or wider, within the bound.
A program may use at most 192 MiB of HBM per device.

v0:
```python
import jax
import jax.numpy as jnp
from jax import lax
from jax.sharding import PartitionSpec as P

BLK = 64
NV = 64
HALO = 4


SCORE_FLOOR = -1e30


def from_behind(x, axis, by):
    count = lax.axis_size(axis)
    pairs = [(i, i + by) for i in range(count) if 0 <= i + by < count]
    return lax.ppermute(x, axis, pairs)


def body(queries, span_kv, cache_kv, verticals, offsets):
    tokens = queries.shape[0]
    heads_kv = span_kv.shape[1]
    row_width = span_kv.shape[2]
    head_depth = row_width // 2
    group_size = queries.shape[1] // (heads_kv * head_depth)
    blocks = tokens // BLK
    owners = lax.axis_size("ctx")
    my_index = lax.axis_index("ctx")
    cache_blocks = cache_kv.shape[0] // BLK
    score_scale = head_depth ** (-0.5)
    query_rows = queries.reshape(tokens, heads_kv, group_size, head_depth)
    cache_blocked = cache_kv.reshape(cache_blocks, BLK, heads_kv, row_width)
    pieces = [span_kv]
    for distance in range(1, HALO + 1):
        pieces.insert(0, from_behind(span_kv, "ctx", distance))
    extended = jnp.concatenate(pieces, 0).reshape((HALO + 1) * blocks, BLK, heads_kv, row_width)
    local_block = jnp.arange(blocks, dtype=jnp.int32)
    source = HALO * blocks + local_block[None, :, None] - offsets[:, None, :]
    global_source = my_index * blocks + local_block[None, :, None] - offsets[:, None, :]
    picked = jnp.stack(
        [extended[source[head_index], :, head_index, :] for head_index in range(heads_kv)], 0
    )
    query_blocks = query_rows.reshape(blocks, BLK, heads_kv, group_size, head_depth)
    slash_scores = (
        jnp.einsum(
            "iqhgd,hiskd->hgiqsk",
            query_blocks,
            picked[..., :head_depth],
            preferred_element_type=jnp.float32,
        )
        * score_scale
    )
    causal = jnp.arange(BLK)[None, :] <= jnp.arange(BLK)[:, None]
    allowed = (global_source >= 0)[:, :, None, :, None] & (
        (offsets[:, None, None, :, None] > 0) | causal[None, None, :, None, :]
    )
    allowed = allowed[:, None]
    slash_scores = jnp.where(allowed, slash_scores, SCORE_FLOOR)
    slash_top = jnp.max(slash_scores, axis=(4, 5))
    slash_weights = jnp.where(allowed, jnp.exp(slash_scores - slash_top[..., None, None]), 0.0)
    slash_total = jnp.sum(slash_weights, axis=(4, 5)).reshape(heads_kv, group_size, tokens)
    slash_weighted = jnp.einsum(
        "hgiqsk,hiskd->hgiqd",
        slash_weights.astype(jnp.bfloat16),
        picked[..., head_depth:],
        preferred_element_type=jnp.float32,
    )
    slash_weighted = slash_weighted.reshape(heads_kv, group_size, tokens, head_depth)
    slash_top = slash_top.reshape(heads_kv, group_size, tokens)
    owner_of = verticals // cache_blocks
    in_owner = verticals % cache_blocks
    is_mine = owner_of == my_index
    capacity = max(2, 2 * NV // owners)
    slot_rank = jnp.cumsum(is_mine.astype(jnp.int32), axis=1) - 1
    slot_hit = is_mine[:, None, :] & (
        slot_rank[:, None, :] == jnp.arange(capacity, dtype=jnp.int32)[None, :, None]
    )
    slot_block = jnp.sum(jnp.where(slot_hit, in_owner[:, None, :], 0), axis=2)
    outgoing = jnp.stack(
        [cache_blocked[slot_block[head_index], :, head_index, :] for head_index in range(heads_kv)],
        2,
    )
    owned_count = jnp.sum(
        (owner_of[:, :, None] == jnp.arange(owners, dtype=jnp.int32)[None, None, :]).astype(
            jnp.int32
        ),
        axis=1,
    )
    shard_rows = lax.all_gather(outgoing, "ctx", axis=0, tiled=True)
    slot_ids = jnp.arange(shard_rows.shape[0], dtype=jnp.int32)
    slot_owner = slot_ids // capacity
    position = slot_ids % capacity
    live_rows = position[:, None] < jnp.transpose(jnp.take(owned_count, slot_owner, axis=1))
    live_rows = jnp.repeat(live_rows, BLK, axis=0)
    key_values = shard_rows.reshape(-1, heads_kv, row_width)
    row_top = jnp.full((heads_kv, group_size, tokens), SCORE_FLOOR, jnp.float32)
    key_rows = key_values[:, :, :head_depth]
    value_rows = key_values[:, :, head_depth:]
    live_mask = jnp.transpose(live_rows)[:, None, None, :]
    scores = (
        jnp.einsum("qhgd,rhd->hgqr", query_rows, key_rows, preferred_element_type=jnp.float32)
        * score_scale
    )
    scores = jnp.where(live_mask, scores, SCORE_FLOOR)
    new_top = jnp.maximum(row_top, jnp.max(scores, axis=-1))
    weights = jnp.where(live_mask, jnp.exp(scores - new_top[..., None]), 0.0)
    row_total = jnp.sum(weights, axis=-1)
    weighted = jnp.einsum(
        "hgqr,rhd->hgqd",
        weights.astype(jnp.bfloat16),
        value_rows,
        preferred_element_type=jnp.float32,
    )
    vertical_state = (new_top, row_total, weighted)
    vertical_top, vertical_total, vertical_weighted = vertical_state
    row_top = jnp.maximum(vertical_top, slash_top)
    vertical_scale = jnp.exp(vertical_top - row_top)
    slash_scale = jnp.exp(slash_top - row_top)
    row_total = vertical_total * vertical_scale + slash_total * slash_scale
    weighted = (
        vertical_weighted * vertical_scale[..., None] + slash_weighted * slash_scale[..., None]
    )
    normalized = weighted / row_total[..., None]
    attended = (
        jnp.transpose(normalized, (2, 0, 1, 3))
        .reshape(tokens, heads_kv * group_size * head_depth)
        .astype(jnp.bfloat16)
    )
    return lax.all_to_all(attended, "head", split_axis=0, concat_axis=1, tiled=True)


def solution(mesh):
    in_specs = (
        P("ctx", "head"),
        P("ctx", "head", None),
        P("ctx", "head", None),
        P("head", None),
        P("head", None),
    )
    out_specs = P(("ctx", "head"), None)
    return jax.shard_map(body, mesh=mesh, in_specs=in_specs, out_specs=out_specs, check_vma=False)
```

profile of v0, /device:TPU:1, one launch (start us, length us, event | category | flops | bytes accessed | tf_op | source)
XLA Modules:
  0.0 208.5 jit_solution(3378839839116987928)
XLA Ops:
  6.5 0.7 fusion.64
  7.2 0.2 reduce_window_sum.11
  7.5 0.7 and_select_fusion.1
  8.2 0.1 fusion.40
  8.4 2.8 %copy.102 = bf16[4096,2,256]{2,0,1:T(8,128)(2,1)S(1)} copy(bf16[4096,2,256]{2,1,0:T(2,128)(2,1)} %param.7) | data formatting | bytes 8388608 | tf_op args[2]
  11.2 2.2 %copy.103 = bf16[64,64,2,256]{3,1,2,0:T(8,128)(2,1)} copy(bf16[64,64,2,256]{3,1,0,2:T(8,128)(2,1)S(1)} %bitcast.131) | data formatting | bytes 8388608 | tf_op jit(solution)/shard_map/reshape | solution.py:32
  13.4 2.7 %gather_fusion.2 = bf16[2,64,256]{2,1,0:T(8,128)(2,1)S(1)} fusion(bf16[64,64,2,256]{3,1,2,0:T(8,128)(2,1)} %copy.103, s32[2]{0:T(128)S(1)} %get-tuple-element.14), kind=kCustom, calls=%fused_computation.2 | custom fusion | bytes 131088 | tf_op jit(solution)/shard_map/gather | solution.py:80
  16.1 2.7 %gather_fusion.1 = bf16[2,64,256]{2,1,0:T(8,128)(2,1)S(1)} fusion(bf16[64,64,2,256]{3,1,2,0:T(8,128)(2,1)} %copy.103, s32[2]{0:T(128)S(1)} %get-tuple-element.13), kind=kCustom, calls=%fused_computation.1 | custom fusion | bytes 131088 | tf_op jit(solution)/shard_map/gather | solution.py:80
  18.9 0.7 pad_maximum_fusion.1
  19.6 4.9 %collective-permute-start.3 = (bf16[128,2,256]{2,0,1:T(8,128)(2,1)S(1)}, bf16[128,2,256]{2,0,1:T(8,128)(2,1)S(1)}, u32[]{:S(2)}, u32[]{:S(2)}) collective-permute-start(bf16[128,2,256]{2,0,1:T(8,128)(2,1)S(1)} %copy.107), channel_id=1, source_target_pairs={{0,4},{4,8},{8,12},{12,16},{16,20},{20,24},{24,28},{28,32},{32,36}... | collective-permute-start | bytes 393224 | tf_op jit(solution)/shard_map/ppermute | solution.py:17
  24.5 3.5 %collective-permute-start.2 = (bf16[128,2,256]{2,0,1:T(8,128)(2,1)S(1)}, bf16[128,2,256]{2,0,1:T(8,128)(2,1)S(1)}, u32[]{:S(2)}, u32[]{:S(2)}) collective-permute-start(bf16[128,2,256]{2,0,1:T(8,128)(2,1)S(1)} %copy.107), channel_id=1, source_target_pairs={{0,8},{4,12},{8,16},{12,20},{16,24},{20,28},{24,32},{28,36},{32,40... | collective-permute-start | bytes 393224 | tf_op jit(solution)/shard_map/ppermute | solution.py:17
  28.1 3.6 %collective-permute-start.1 = (bf16[128,2,256]{2,0,1:T(8,128)(2,1)S(1)}, bf16[128,2,256]{2,0,1:T(8,128)(2,1)S(1)}, u32[]{:S(2)}, u32[]{:S(2)}) collective-permute-start(bf16[128,2,256]{2,0,1:T(8,128)(2,1)S(1)} %copy.107), channel_id=1, source_target_pairs={{0,12},{4,16},{8,20},{12,24},{16,28},{20,32},{24,36},{28,40},{32,4... | collective-permute-start | bytes 393224 | tf_op jit(solution)/shard_map/ppermute | solution.py:17
  31.7 5.2 %collective-permute-start = (bf16[128,2,256]{2,0,1:T(8,128)(2,1)S(1)}, bf16[128,2,256]{2,0,1:T(8,128)(2,1)S(1)}, u32[]{:S(2)}, u32[]{:S(2)}) collective-permute-start(bf16[128,2,256]{2,0,1:T(8,128)(2,1)S(1)} %copy.107), channel_id=1, source_target_pairs={{0,16},{4,20},{8,24},{12,28},{16,32},{20,36},{24,40},{28,44},{32,4... | collective-permute-start | bytes 393224 | tf_op jit(solution)/shard_map/ppermute | solution.py:17
  37.1 0.6 gather_fusion
  38.1 0.1 broadcast_or_fusion
  38.2 0.2 broadcast_and_fusion
  38.7 0.1 reshape.283
  38.9 1.3 collective-permute-done
  40.4 0.6 gather_fusion.4
  41.0 0.6 gather_fusion.3
  41.6 5.1 %fusion.8 = (f32[2,8,2,64]{3,1,2,0:T(8,128)S(1)}, f32[2,2,8,64,64,8]{4,3,5,2,1,0:T(8,128)}) fusion(pred[2,2,64,8,64]{2,4,3,1,0:T(8,128)(4,1)S(1)} %broadcast_and_fusion, bf16[2,64,2,8,128,1]{4,3,2,1,0,5:T(8,128)(2,1)S(1)} %bitcast.135, bf16[1,2,8,64,256]{4,3,2,1,0:T(8,128)(2,1)S(1)} %bitcast.139, bf16[1,2,8,64,256]{4,3,2,1,0:T(8,128)(2,1)S(1)} %bitcast.137), kind=kOutput, calls=%fused_computation.17 | convolution fusion | flops 272627712 | bytes 5906432 | tf_op jit(solution)/shard_map/iqhgd,hiskd->hgiqsk/dot_general | solution.py:45
  46.8 4.8 %fusion.9 = f32[2,8,2,64]{3,1,2,0:T(8,128)S(1)} fusion(f32[2,2,8,64,64,8]{4,3,5,2,1,0:T(8,128)} %get-tuple-element.16, f32[2,8,2,64]{3,1,2,0:T(8,128)S(1)} %get-tuple-element.15, pred[2,2,64,8,64]{2,4,3,1,0:T(8,128)(4,1)S(1)} %broadcast_and_fusion), kind=kLoop, calls=%fused_computation.18 | loop fusion | flops 5240832 | bytes 4341760 | tf_op jit(solution)/shard_map/reduce_sum | solution.py:61
  51.7 5.6 %fusion.21 = f32[2,8,2,64,128]{4,3,1,2,0:T(8,128)S(1)} fusion(f32[2,2,8,64,64,8]{4,3,5,2,1,0:T(8,128)} %get-tuple-element.16, f32[2,8,2,64]{3,1,2,0:T(8,128)S(1)} %get-tuple-element.15, pred[2,2,64,8,64]{2,4,3,1,0:T(8,128)(4,1)S(1)} %broadcast_and_fusion, bf16[1,2,8,64,256]{4,3,2,1,0:T(8,128)(2,1)S(1)} %bitcast.138, ...), kind=kOutput, calls=%fused_computation.27 | convolution fusion | flops 274726912 | bytes 6430720 | tf_op jit(solution)/shard_map/hgiqsk,hiskd->hgiqd/dot_general | solution.py:62
  57.4 50.8 %all-gather.2.cloned.1.call-done = bf16[128,64,2,256]{3,1,0,2:T(8,128)(2,1)} async-done(((bf16[2,64,2,256]{3,1,0,2:T(8,128)(2,1)}), bf16[128,64,2,256]{3,1,0,2:T(8,128)(2,1)}) %all-gather.2.cloned.1.call-update) | async-done | bytes 8388624 | tf_op jit(solution)/shard_map/all_gather | solution.py:89
  108.2 25.1 %bitcast_reduce_fusion = (f32[2,8,128]{2,1,0:T(8,128)S(1)}, f32[2,8192,128,8]{2,1,3,0:T(8,128)}) fusion(pred[2,8192]{1,0:T(4,128)(4,1)S(1)} %bitcast.141, bf16[128,2,8,128]{3,2,1,0:T(8,128)(2,1)S(1)} %bitcast.136, bf16[8192,2,256]{2,0,1:T(8,128)(2,1)} %bitcast.146), kind=kOutput, calls=%fused_computation.6 | convolution fusion | flops 4345296896 | bytes 71852032 | tf_op jit(solution)/shard_map/qhgd,rhd->hgqr/dot_general | solution.py:101
  133.3 21.5 %fusion.2 = f32[2,8,128]{2,1,0:T(8,128)S(1)} fusion(f32[2,8192,128,8]{2,1,3,0:T(8,128)} %get-tuple-element.18, f32[2,8,128]{2,1,0:T(8,128)S(1)} %broadcast_maximum_fusion, pred[2,8192]{1,0:T(4,128)(4,1)S(1)} %bitcast.142), kind=kLoop, calls=%fused_computation.10 | loop fusion | flops 83884032 | bytes 67141632 | tf_op jit(solution)/shard_map/reduce_sum | solution.py:107
  154.9 0.3 bitcast_multiply_fusion
  155.2 32.2 %fusion.26 = bf16[128,2,8,128]{3,0,2,1:T(8,128)(2,1)S(1)} fusion(f32[2,8,128,128]{3,2,1,0:T(8,128)S(1)} %bitcast_multiply_fusion, bf16[8192,2,256]{2,0,1:T(8,128)(2,1)} %bitcast.147, f32[2,8192,128,8]{2,1,3,0:T(8,128)} %get-tuple-element.18, f32[2,8,128]{2,1,0:T(8,128)S(1)} %broadcast_maximum_fusion, pred[2,8192]{1,0:T(4,128)(4,1)S(1)} %bitcast.143, ...), kind=kOutput, calls=%fused_computation.32 | convolution fusion | flops 4379901952 | bytes 72966144 | tf_op jit(solution)/shard_map/hgqr,rhd->hgqd/dot_general | solution.py:108
  187.4 0.3 copy.119
  187.8 0.2 convert_element_type.28
  188.0 12.8 %all_to_all.16 = bf16[4,32,2048]{2,1,0:T(8,128)(2,1)S(1)} all-to-all(bf16[4,32,2048]{2,1,0:T(8,128)(2,1)S(1)} %convert_element_type.28), channel_id=1, replica_groups=mesh['ctx'=64,'head'=4] {'head'}, dimensions={0} | all-to-all | bytes 1048576 | tf_op jit(solution)/shard_map/all_to_all | solution.py:129
  200.8 0.8 copy.132
  (45 shorter events, 1.3 us)
Async XLA Ops:
  6.5 101.6 %all-gather.2.cloned.1.call-start = ((), (), s32[]{:S(2)}) async-start(), calls=%async_computation.1 | async-start | bytes 8519680 | tf_op jit(solution)/shard_map/all_gather | solution.py:89
  8.3 11.3 %copy-start.1 = (bf16[128,2,256]{2,1,0:T(2,128)(2,1)S(1)}, bf16[128,2,256]{2,1,0:T(2,128)(2,1)}, u32[]{:S(2)}) copy-start(bf16[128,2,256]{2,1,0:T(2,128)(2,1)} %param.6) | copy-start | bytes 393220
  8.3 29.5 %copy-start.2 = (s32[2,8]{1,0:T(2,128)S(1)}, s32[2,8]{1,0:T(2,128)}, u32[]{:S(2)}) copy-start(s32[2,8]{1,0:T(2,128)} %param.9) | copy-start | bytes 196
  8.3 30.5 %copy-start = (bf16[128,2048]{1,0:T(8,128)(2,1)S(1)}, bf16[128,2048]{1,0:T(8,128)(2,1)}, u32[]{:S(2)}) copy-start(bf16[128,2048]{1,0:T(8,128)(2,1)} %param.5) | copy-start | bytes 1572868
  19.6 20.7 %collective-permute-start.3 = (bf16[128,2,256]{2,0,1:T(8,128)(2,1)S(1)}, bf16[128,2,256]{2,0,1:T(8,128)(2,1)S(1)}, u32[]{:S(2)}, u32[]{:S(2)}) collective-permute-start(bf16[128,2,256]{2,0,1:T(8,128)(2,1)S(1)} %copy.107), channel_id=1, source_target_pairs={{0,4},{4,8},{8,12},{12,16},{16,20},{20,24},{24,28},{28,32},{32,36}... | collective-permute-start | bytes 393224 | tf_op jit(solution)/shard_map/ppermute | solution.py:17
  24.5 15.7 %collective-permute-start.2 = (bf16[128,2,256]{2,0,1:T(8,128)(2,1)S(1)}, bf16[128,2,256]{2,0,1:T(8,128)(2,1)S(1)}, u32[]{:S(2)}, u32[]{:S(2)}) collective-permute-start(bf16[128,2,256]{2,0,1:T(8,128)(2,1)S(1)} %copy.107), channel_id=1, source_target_pairs={{0,8},{4,12},{8,16},{12,20},{16,24},{20,28},{24,32},{28,36},{32,40... | collective-permute-start | bytes 393224 | tf_op jit(solution)/shard_map/ppermute | solution.py:17
  28.1 12.1 %collective-permute-start.1 = (bf16[128,2,256]{2,0,1:T(8,128)(2,1)S(1)}, bf16[128,2,256]{2,0,1:T(8,128)(2,1)S(1)}, u32[]{:S(2)}, u32[]{:S(2)}) collective-permute-start(bf16[128,2,256]{2,0,1:T(8,128)(2,1)S(1)} %copy.107), channel_id=1, source_target_pairs={{0,12},{4,16},{8,20},{12,24},{16,28},{20,32},{24,36},{28,40},{32,4... | collective-permute-start | bytes 393224 | tf_op jit(solution)/shard_map/ppermute | solution.py:17
  31.7 8.5 %collective-permute-start = (bf16[128,2,256]{2,0,1:T(8,128)(2,1)S(1)}, bf16[128,2,256]{2,0,1:T(8,128)(2,1)S(1)}, u32[]{:S(2)}, u32[]{:S(2)}) collective-permute-start(bf16[128,2,256]{2,0,1:T(8,128)(2,1)S(1)} %copy.107), channel_id=1, source_target_pairs={{0,16},{4,20},{8,24},{12,28},{16,32},{20,36},{24,40},{28,44},{32,4... | collective-permute-start | bytes 393224 | tf_op jit(solution)/shard_map/ppermute | solution.py:17
Sparse Core Ops, SparseCore 0:
  19.7 88.4 all-gather.1
where the time goes:
time: 209 us
  matrix products  68.1 us (33%)
  waiting for transfers between devices  52 us (25%)
  other arithmetic  29.8 us (14%)
  starting transfers between devices  17.2 us (8%)
  local copies, waits for them, and re-layouts  14.8 us (7%)
  between operations  13.8 us (7%)
  blocking collectives  12.8 us (6%)
    all_gather x1, waiting for transfers between devices, body(): shard_rows = lax.all_gather(outgoing, 'ctx', axis=0, tiled=True)  50.8 us
    dot_general x1, matrix products, body(): jnp.einsum('hgqr,rhd->hgqd', weights.astype(jnp.bfloat16), value_rows, pr...  32.2 us
    dot_general x1, matrix products, body(): jnp.einsum('qhgd,rhd->hgqr', query_rows, key_rows, preferred_element_type...  25.1 us
    reduce_sum x1, other arithmetic, body(): row_total = jnp.sum(weights, axis=-1)  21.5 us
    ppermute x4, starting transfers between devices, from_behind(): return lax.ppermute(x, axis, pairs)  17.2 us
    all_to_all x1, blocking collectives, body(): lax.all_to_all(attended, 'head', split_axis=0, concat_axis=1, tiled=True)  12.8 us
    dot_general x1, matrix products, body(): jnp.einsum('hgiqsk,hiskd->hgiqd', slash_weights.astype(jnp.bfloat16), pic...  5.63 us
    gather x2, local copies, waits for them, and re-layouts, body(): cache_blocked[slot_block[head_index], :, head_index, :]  5.48 us
  transfers between devices with their start and end apart: 5, of which 2 were waited for; matrix products, arithmetic and copies ran while one was open for 9% of the time, Pallas kernels for 0%

commit v1 on v0

v1 whole, which is shorter than its diff:
```python
import jax
import jax.numpy as jnp
from jax import lax
from jax.experimental import pallas as pl
from jax.experimental.pallas import tpu as pltpu
from jax.sharding import PartitionSpec as P

BLK = 64
HD = 128
NX, NZ, NY = 4, 8, 4
CHIPS = NX * NZ
GROUP = 8
TOK = 128
SUB = TOK // NY
ROWS = GROUP * SUB
CHUNKS = 2 * NY
CHUNK_KEYS = 4 * BLK
TILE = NX * CHUNK_KEYS
WINDOW = 6 * TOK
QW = GROUP * HD
FLOOR = -1e30
DEAD = -30000.0
SCALE = float(HD ** -0.5 * 1.4426950408889634)
MESH = pl.DeviceIdType.MESH


def kernel(picks, bias, q_hbm, span_hbm, cache_hbm, out_hbm,
           cache, span, span_heads, staged, gathered, q_own, q_far, window,
           q2, k2, v2, wk, wv, acc, top, slab,
           load_sem, swap_send, swap_recv, halo_send, halo_recv,
           piece_send, piece_recv, out_send, out_recv, own_sem):
    me = lax.axis_index("ctx")
    y = lax.axis_index("head")
    chip = me // 2
    core = me % 2
    other = 1 - core
    x = chip // NZ
    z = chip % NZ

    def at_chip(cx, cz, which):
        return (2 * ((cx % NX) * NZ + cz % NZ) + which, y)

    partner = (2 * chip + other, y)
    x_up, x_down, x_far = (at_chip(x + s, z, core) for s in (1, NX - 1, 2))
    z_up, z_down = (at_chip(x, z + s, core) for s in (1, NZ - 1))

    def linear(step, which):
        return (2 * ((chip + CHIPS + step) % CHIPS) + which, y)

    barrier = pltpu.get_barrier_semaphore()
    peers = [partner, x_up, x_down, x_far, z_up, z_down]
    peers += [linear(s, w) for s in (1, -1, 2, -2) for w in (0, 1)]
    peers += [(2 * chip + w, (y + r) % NY) for r in (1, 2, 3) for w in (0, 1)]
    for peer in peers:
        pl.semaphore_signal(barrier, inc=1, device_id=peer, device_id_type=MESH)

    load_cache = pltpu.make_async_copy(cache_hbm, cache, load_sem.at[0])
    load_span = pltpu.make_async_copy(span_hbm, span, load_sem.at[1])
    own_columns = pl.ds(pl.multiple_of(core * QW, QW), QW)
    far_columns = pl.ds(pl.multiple_of(other * QW, QW), QW)
    load_q = pltpu.make_async_copy(q_hbm.at[:, own_columns], q_own, load_sem.at[2])
    load_span.start()
    load_cache.start()
    load_q.start()

    load_span.wait()
    both = span[...].astype(jnp.float32)
    for head in range(2):
        span_heads[head] = both[:, head, :].astype(jnp.bfloat16)
    load_cache.wait()
    for head in range(2):
        for slot in range(2):
            block = cache[picks[head, slot]].astype(jnp.float32)
            staged[head, slot * BLK:(slot + 1) * BLK, :] = block[:, head, :].astype(jnp.bfloat16)

    mine = pl.ds(pl.multiple_of(core * 2 * BLK, 2 * BLK), 2 * BLK)
    gathered[z, x, mine, :] = staged[core]
    own_rows = pl.ds(pl.multiple_of(4 * TOK + core * TOK, TOK), TOK)
    window[own_rows, :] = span_heads[core]

    pl.semaphore_wait(barrier, len(peers))

    def remote(src, dst, send, recv, device):
        return pltpu.make_async_remote_copy(
            src_ref=src, dst_ref=dst, send_sem=send, recv_sem=recv,
            device_id=device, device_id_type=MESH)

    swaps = [
        remote(staged.at[other], gathered.at[z, x, mine, :], swap_send.at[0], swap_recv.at[0], partner),
        remote(q_hbm.at[:, far_columns], q_far, swap_send.at[1], swap_recv.at[1], partner),
        remote(span_heads.at[other], window.at[own_rows, :], swap_send.at[2], swap_recv.at[2], partner),
    ]
    for swap in swaps:
        swap.start()
    halos = []
    for back in (1, 2):
        rows = pl.ds(pl.multiple_of((2 - back) * 2 * TOK + core * TOK, TOK), TOK)
        for head in range(2):
            halos.append(remote(
                span_heads.at[head], window.at[rows, :],
                halo_send.at[back - 1, head], halo_recv.at[back - 1, core],
                linear(back, head)))

    def row_of(k):
        return (z + NZ + (1 - 2 * (k % 2)) * ((k + 1) // 2)) % NZ

    def piece(k, off, way, device, k_there, off_there):
        src = gathered.at[row_of(k), (x + off) % NX]
        return remote(src, src, piece_send.at[k, off, way],
                      piece_recv.at[k_there, off_there], device)

    def along_z(k, off, act):
        @pl.when(k == 0)
        def _():
            act(piece(k, off, 0, z_up, 1, off))
            act(piece(k, off, 1, z_down, 2, off))

        @pl.when((k % 2 == 1) & (k <= 3))
        def _():
            act(piece(k, off, 0, z_up, k + 2, off))

        @pl.when((k % 2 == 0) & (k >= 2))
        def _():
            act(piece(k, off, 1, z_down, k + 2 - k // 6, off))

    def along_x(k, act):
        act(piece(k, 0, 2, x_up, k, 3))
        act(piece(k, 0, 3, x_down, k, 1))

        @pl.when(k == 0)
        def _():
            act(piece(k, 0, 4, x_far, k, 2))

    def relay_x(k, act):
        @pl.when(k % 2 == 1)
        def _():
            act(piece(k, 3, 2, x_up, k, 2))

        @pl.when((k % 2 == 0) & (k >= 2))
        def _():
            act(piece(k, 1, 3, x_down, k, 2))

    def begin(copy):
        copy.start()

    def drain(copy):
        copy.wait_send()

    def arrive(k, off):
        here = gathered.at[row_of(k), (x + off) % NX]
        remote(here, here, piece_send.at[k, off, 0], piece_recv.at[k, off], partner).wait_recv()

    def stage_a(k):
        arrive(k, 0)
        along_z(k, 0, begin)
        along_x(k, begin)

    def stage_b(k):
        @pl.when(k % 2 == 1)
        def _():
            arrive(k, 3)

        @pl.when(k % 2 == 0)
        def _():
            arrive(k, 1)
        relay_x(k, begin)

    swaps[0].wait_recv()
    along_z(0, 0, begin)
    along_x(0, begin)
    for halo in halos:
        halo.start()

    load_q.wait()
    swaps[1].wait_recv()
    for rel in range(2):
        source = q_own if rel == 0 else q_far
        for r in range(NY):
            first = pl.multiple_of(((y + r) % NY) * SUB, SUB)
            for h in range(GROUP):
                part = source[pl.ds(first, SUB), h * HD:(h + 1) * HD].astype(jnp.float32) * SCALE
                high = part.astype(jnp.bfloat16)
                low = (part - high.astype(jnp.float32)).astype(jnp.bfloat16)
                lane = lax.broadcasted_iota(jnp.int32, (SUB, HD), 1)
                low = jnp.where(lane == HD - 1, jnp.ones_like(low), low)
                base = (rel * NY + r) * ROWS + h * SUB
                q2[base:base + SUB, 0:HD] = high
                q2[base:base + SUB, HD:2 * HD] = low

    acc[...] = jnp.zeros_like(acc)
    top[...] = jnp.full_like(top, FLOOR)
    v2[:, HD:2 * HD] = jnp.ones((TILE, HD), jnp.bfloat16)
    wv[:, HD:2 * HD] = jnp.ones((WINDOW, HD), jnp.bfloat16)

    def update(n, scores, values):
        rows = slice(n * ROWS, (n + 1) * ROWS)
        before = top[rows, :]
        now = jnp.maximum(before, jnp.max(scores, axis=1, keepdims=True))
        weights = jnp.exp2(scores - now[:, 0:1]).astype(jnp.bfloat16)
        added = jnp.dot(weights, values, preferred_element_type=jnp.float32)
        keep = jnp.exp2(before - now)
        top[rows, :] = now
        acc[rows, 0:HD] = acc[rows, 0:HD] * keep + added[:, 0:HD]
        acc[rows, HD:2 * HD] = acc[rows, HD:2 * HD] * keep + added[:, HD:2 * HD]

    def score(n, keys):
        return lax.dot_general(
            q2[n * ROWS:(n + 1) * ROWS, :], keys, (((1,), (1,)), ((), ())),
            preferred_element_type=jnp.float32)

    def slash():
        for back in (1, 2):
            for which in range(2):
                rows = window.at[(2 - back) * 2 * TOK + which * TOK:(2 - back) * 2 * TOK + (which + 1) * TOK, :]
                remote(rows, rows, halo_send.at[back - 1, 0], halo_recv.at[back - 1, which], partner).wait_recv()
        swaps[2].wait_recv()
        wk[:, 0:HD] = window[:, 0:HD]
        lane = lax.broadcasted_iota(jnp.int32, (WINDOW, HD), 1)
        wk[:, HD:2 * HD] = jnp.where(lane == HD - 1, jnp.zeros((WINDOW, HD), jnp.bfloat16), window[:, 0:HD])
        wv[:, 0:HD] = window[:, HD:2 * HD]
        for n in range(CHUNKS):
            place = core if n < NY else other
            first = ((y + n % NY) % NY) * SUB
            block = 2 * place + first // BLK
            keys = pl.ds(pl.multiple_of((block + 1) * BLK, BLK), 8 * BLK)
            column = lax.broadcasted_iota(jnp.int32, (ROWS, 8 * BLK), 1)
            token = lax.broadcasted_iota(jnp.int32, (ROWS, 8 * BLK), 0) % SUB + first % BLK
            allowed = (column <= 7 * BLK + token) & (column >= (7 - block - 4 * chip) * BLK)
            scores = jnp.where(allowed, score(n, wk[keys, :]), FLOOR)
            update(n, scores, wv[keys, :])

    def tile(k):
        row = row_of(k)
        lane = lax.broadcasted_iota(jnp.int32, (BLK, HD), 1)
        for cx in range(NX):
            for b in range(4):
                owner = 2 * (cx * NZ + row) + b // 2
                fill = jnp.full((BLK, HD), bias[core, 2 * owner + b % 2], jnp.float32)
                rows = slice(b * BLK, (b + 1) * BLK)
                there = slice(cx * CHUNK_KEYS + b * BLK, cx * CHUNK_KEYS + (b + 1) * BLK)
                keys = gathered[row, cx, rows, 0:HD]
                k2[there, 0:HD] = keys
                k2[there, HD:2 * HD] = jnp.where(lane == HD - 1, fill.astype(jnp.bfloat16), keys)
                v2[there, 0:HD] = gathered[row, cx, rows, HD:2 * HD]
        for n in range(CHUNKS):
            update(n, score(n, k2[...]), v2[...])

    @pl.when(core == 1)
    def _():
        stage_a(1)

    def step(k, carry):
        @pl.when(core == 0)
        def _():
            @pl.when(k > 0)
            def _():
                arrive(k, 0)
                along_z(k, 0, begin)
            for off in (1, 3, 2):
                arrive(k, off)
                along_z(k, off, begin)

        @pl.when(core == 1)
        def _():
            @pl.when(k + 2 < NZ)
            def _():
                stage_a(k + 2)

            @pl.when(k + 1 < NZ)
            def _():
                stage_b(k + 1)

            @pl.when((k == 0) | (k % 2 == 1))
            def _():
                arrive(k, 1)

            @pl.when(k % 2 == 0)
            def _():
                arrive(k, 3)
            arrive(k, 2)
        tile(k)

        @pl.when(k == 0)
        def _():
            slash()
        return carry

    lax.fori_loop(0, NZ, step, 0)

    out_columns = pl.ds(pl.multiple_of(y * 2 * QW + core * QW, QW), QW)
    sends = []
    keep_own = pltpu.make_async_copy(slab.at[0], out_hbm.at[:, out_columns], own_sem)
    for n in (2, 6, 1, 5, 3, 7, 4, 0):
        rows = slice(n * ROWS, (n + 1) * ROWS)
        done = (acc[rows, 0:HD] / acc[rows, HD:2 * HD]).astype(jnp.bfloat16)
        for h in range(GROUP):
            slab[n, :, h * HD:(h + 1) * HD] = done[h * SUB:(h + 1) * SUB, :]
        if n == 0:
            keep_own.start()
        else:
            place = core if n < NY else other
            send = remote(slab.at[n], out_hbm.at[:, out_columns], out_send.at[n], out_recv.at[n],
                          (2 * chip + place, (y + n % NY) % NY))
            send.start()
            sends.append(send)

    for swap in swaps:
        swap.wait_send()
    for halo in halos:
        halo.wait_send()

    def finish(k, carry):
        along_z(k, 0, drain)

        @pl.when(core == 0)
        def _():
            for off in (1, 2, 3):
                along_z(k, off, drain)

            @pl.when(k == 0)
            def _():
                along_x(k, drain)

        @pl.when(core == 1)
        def _():
            along_x(k, drain)
            relay_x(k, drain)
        return carry

    lax.fori_loop(0, NZ, finish, 0)
    for send in sends:
        send.wait()
    keep_own.wait()


def body(queries, span_kv, cache_kv, verticals, offsets):
    heads = span_kv.shape[1]
    owners = lax.axis_size("ctx")
    my_index = lax.axis_index("ctx")
    cache_blocks = cache_kv.shape[0] // BLK
    owner_of = verticals // cache_blocks
    in_owner = verticals % cache_blocks
    is_mine = owner_of == my_index
    rank = jnp.cumsum(is_mine.astype(jnp.int32), axis=1) - 1
    slots = jnp.arange(2, dtype=jnp.int32)
    hit = is_mine[:, None, :] & (rank[:, None, :] == slots[None, :, None])
    picks = jnp.sum(jnp.where(hit, in_owner[:, None, :], 0), axis=2)
    held = jnp.sum(
        (owner_of[:, None, :] == jnp.arange(owners, dtype=jnp.int32)[None, :, None]).astype(jnp.int32),
        axis=2)
    bias = jnp.where(slots[None, None, :] < held[:, :, None], 0.0, DEAD).astype(jnp.float32)
    bias = bias.reshape(heads, 2 * owners)
    bf16 = jnp.bfloat16
    any_space = pl.BlockSpec(memory_space=pl.ANY)
    smem = pl.BlockSpec(memory_space=pltpu.SMEM)
    dma = pltpu.SemaphoreType.DMA
    return pl.pallas_call(
        kernel,
        out_shape=jax.ShapeDtypeStruct((SUB, 4 * 2 * QW), bf16),
        in_specs=[smem, smem, any_space, any_space, any_space],
        out_specs=any_space,
        scratch_shapes=[
            pltpu.VMEM((cache_blocks, BLK) + cache_kv.shape[1:], bf16),
            pltpu.VMEM(span_kv.shape, bf16),
            pltpu.VMEM((2, TOK, 2 * HD), bf16),
            pltpu.VMEM((2, 2 * BLK, 2 * HD), bf16),
            pltpu.VMEM((NZ, NX, CHUNK_KEYS, 2 * HD), bf16),
            pltpu.VMEM((TOK, QW), bf16),
            pltpu.VMEM((TOK, QW), bf16),
            pltpu.VMEM((WINDOW, 2 * HD), bf16),
            pltpu.VMEM((CHUNKS * ROWS, 2 * HD), bf16),
            pltpu.VMEM((TILE, 2 * HD), bf16),
            pltpu.VMEM((TILE, 2 * HD), bf16),
            pltpu.VMEM((WINDOW, 2 * HD), bf16),
            pltpu.VMEM((WINDOW, 2 * HD), bf16),
            pltpu.VMEM((CHUNKS * ROWS, 2 * HD), jnp.float32),
            pltpu.VMEM((CHUNKS * ROWS, HD), jnp.float32),
            pltpu.VMEM((CHUNKS, SUB, QW), bf16),
            dma((3,)), dma((3,)), dma((3,)), dma((2, 2)), dma((2, 2)),
            dma((NZ, NX, 5)), dma((NZ, NX)), dma((CHUNKS,)), dma((CHUNKS,)), dma,
        ],
        compiler_params=pltpu.CompilerParams(
            collective_id=0, has_side_effects=True, vmem_limit_bytes=60 << 20),
    )(picks, bias, queries, span_kv, cache_kv.reshape((cache_blocks, BLK) + cache_kv.shape[1:]))


def solution(mesh):
    in_specs = (
        P("ctx", "head"),
        P("ctx", "head", None),
        P("ctx", "head", None),
        P("head", None),
        P("head", None),
    )
    out_specs = P(("ctx", "head"), None)
    return jax.shard_map(body, mesh=mesh, in_specs=in_specs, out_specs=out_specs, check_vma=False)
```

time: 209 us -> 76.8 us (0.37)
  Pallas kernels: 0 us -> 71.3 us
  matrix products: 68.1 us -> 0 us
  waiting for transfers between devices: 52 us -> 0 us
  other arithmetic: 29.8 us -> 3.05 us
  starting transfers between devices: 17.2 us -> 0 us
  between operations: 13.8 us -> 0.02 us
  blocking collectives: 12.8 us -> 0 us
  local copies, waits for them, and re-layouts: 14.8 us -> 2.24 us
    pallas_call x0 -> x1, Pallas kernels: none -> 71.3 us  [body(): pl.pallas_call(kernel, out_shape=jax.ShapeDtypeStruct((SUB, 4 * 2 * QW),...]
    dot_general x4 -> x0, matrix products: 68.1 us -> none  [the longest x1 32.2 us: body(): jnp.einsum('hgqr,rhd->hgqd', weights.astype(jnp.bfloat16), value_rows, pr...]
    all_gather x1 -> x0, waiting for transfers between devices: 50.8 us -> none  [body(): shard_rows = lax.all_gather(outgoing, 'ctx', axis=0, tiled=True)]
    reduce_sum x4 -> x2, other arithmetic: 26.6 us -> 0.82 us  [the longest x1 0.71 us: body(): picks = jnp.sum(jnp.where(hit, in_owner[:, None, :], 0), axis=2)]
    ppermute x4 -> x0, starting transfers between devices: 17.2 us -> none  [from_behind(): return lax.ppermute(x, axis, pairs)]
    all_to_all x1 -> x0, blocking collectives: 12.8 us -> none  [body(): lax.all_to_all(attended, 'head', split_axis=0, concat_axis=1, tiled=True)]
    gather x6 -> x0, local copies, waits for them, and re-layouts: 7.35 us -> none  [the longest x2 5.48 us: body(): cache_blocked[slot_block[head_index], :, head_index, :]]
    reshape x5 -> x0, local copies, waits for them, and re-layouts: 2.56 us -> none  [the longest x1 2.23 us: body(): cache_blocked = cache_kv.reshape(cache_blocks, BLK, heads_kv, row_width)]
  transfers between devices with their start and end apart: 5 -> 0, of which waited for: 2 -> 0; matrix products, arithmetic and copies ran while one was open for 9% -> 0% of each run, Pallas kernels for 0% -> 0%
where the time goes in v1:
time: 76.8 us; the launch traced here: 76.6 us
  Pallas kernels  71.3 us (93%)
  other arithmetic  3.05 us (4%)
  local copies, waits for them, and re-layouts  2.24 us (3%)
    pallas_call x1, Pallas kernels, body(): pl.pallas_call(kernel, out_shape=jax.ShapeDtypeStruct((SUB, 4 * 2 * QW),...  71.3 us
    unnamed x1, local copies, waits for them, and re-layouts  1.87 us

profile of v1, /device:TPU:1, one launch (start us, length us, event | category | flops | bytes accessed | tf_op | source)
XLA Modules:
  0.0 76.6 jit_solution(14178214118491156429)
XLA Ops:
  0.0 0.7 fusion.1
  0.7 0.2 reduce_window_sum.11
  0.9 0.1 convert_reduce_fusion
  1.0 0.7 and_select_fusion.1
  1.7 0.7 fusion.picks
  2.5 0.1 lt.28
  2.6 0.1 lt.30
  2.7 0.2 lt.31
  2.8 0.6 compare_select_fusion.bias
  3.4 71.3 %shard_map.46 = bf16[32,8192]{1,0:T(8,128)(2,1)} custom-call(s32[2,2]{1,0:T(2,128)} %fusion.picks, f32[2,128]{1,0:T(2,128)} %compare_select_fusion.bias, bf16[128,2048]{1,0:T(8,128)(2,1)} %q_hbm.1, bf16[128,2,256]{2,1,0:T(2,128)(2,1)} %span_hbm.1, bf16[64,64,2,256]{3,2,1,0:T(2,128)(2,1)} %bitcast.1), custom_call_target="tpu_custom_call" | custom-call | tf_op jit(solution)/shard_map/pallas_call | solution.py:357
  74.7 1.9 %copy.6 = bf16[32,8192]{1,0:T(8,128)(2,1)} copy(bf16[32,8192]{1,0:T(8,128)(2,1)} %shard_map.46) | data formatting | bytes 1048576
  (1 shorter events, 0.0 us)

commit v2 on v1

--- a/solution.py
+++ b/solution.py
@@ -16,7 +16,9 @@
 CHUNKS = 2 * NY
 CHUNK_KEYS = 4 * BLK
 TILE = NX * CHUNK_KEYS
-WINDOW = 6 * TOK
+FAR = 2 * TOK
+WINDOW = 3 * FAR
+NV = 64
 QW = GROUP * HD
 FLOOR = -1e30
 DEAD = -30000.0
@@ -24,10 +26,10 @@
 MESH = pl.DeviceIdType.MESH
 
 
-def kernel(picks, bias, q_hbm, span_hbm, cache_hbm, out_hbm,
-           cache, span, span_heads, staged, gathered, q_own, q_far, window,
+def kernel(verts_hbm, q_hbm, span_hbm, cache_hbm, out_hbm,
+           verts, bias, cache, span, span_heads, staged, gathered, q_own, q_far, window,
            q2, k2, v2, wk, wv, acc, top, slab,
-           load_sem, swap_send, swap_recv, halo_send, halo_recv,
+           load_sem, swap_send, swap_recv, halo_send, halo_recv, ready,
            piece_send, piece_recv, out_send, out_recv, own_sem):
     me = lax.axis_index("ctx")
     y = lax.axis_index("head")
@@ -43,14 +45,13 @@
     partner = (2 * chip + other, y)
     x_up, x_down, x_far = (at_chip(x + s, z, core) for s in (1, NX - 1, 2))
     z_up, z_down = (at_chip(x, z + s, core) for s in (1, NZ - 1))
-
-    def linear(step, which):
-        return (2 * ((chip + CHIPS + step) % CHIPS) + which, y)
-
+    after, before_it = ((2 * ((chip + CHIPS + s) % CHIPS) + core, y) for s in (1, -1))
+
+    load_verts = pltpu.make_async_copy(verts_hbm, verts, load_sem.at[3])
+    load_verts.start()
     barrier = pltpu.get_barrier_semaphore()
-    peers = [partner, x_up, x_down, x_far, z_up, z_down]
-    peers += [linear(s, w) for s in (1, -1, 2, -2) for w in (0, 1)]
-    peers += [(2 * chip + w, (y + r) % NY) for r in (1, 2, 3) for w in (0, 1)]
+    peers = [partner, x_up, x_down, z_up, z_down, after, before_it]
+    peers += [(2 * chip + w, (y + r) % NY) for r in (1, 3) for w in (0, 1)]
     for peer in peers:
         pl.semaphore_signal(barrier, inc=1, device_id=peer, device_id_type=MESH)
 
@@ -63,6 +64,17 @@
     load_cache.start()
     load_q.start()
 
+    load_verts.wait()
+    mine_at = (verts[...] // BLK) == me
+    within = verts[...] % BLK
+    most = jnp.where(mine_at, within, 0)
+    least = jnp.where(mine_at, within, BLK - 1)
+    owner_row = verts[pl.ds(core, 1), :] // BLK
+    owner_index = lax.broadcasted_iota(jnp.int32, (2 * CHIPS, NV), 0)
+    held = jnp.sum(jnp.where(owner_index == owner_row, 1.0, 0.0), axis=1, keepdims=True)
+    for slot in range(2):
+        dead = jnp.where(held > slot + 0.5, 0.0, DEAD)
+        bias[slot] = jnp.broadcast_to(dead, (2 * CHIPS, HD))
     load_span.wait()
     both = span[...].astype(jnp.float32)
     for head in range(2):
@@ -70,7 +82,8 @@
     load_cache.wait()
     for head in range(2):
         for slot in range(2):
-            block = cache[picks[head, slot]].astype(jnp.float32)
+            pick = jnp.max(most[head:head + 1]) if slot == 0 else jnp.min(least[head:head + 1])
+            block = cache[pick].astype(jnp.float32)
             staged[head, slot * BLK:(slot + 1) * BLK, :] = block[:, head, :].astype(jnp.bfloat16)
 
     mine = pl.ds(pl.multiple_of(core * 2 * BLK, 2 * BLK), 2 * BLK)
@@ -79,6 +92,8 @@
     window[own_rows, :] = span_heads[core]
 
     pl.semaphore_wait(barrier, len(peers))
+    pl.semaphore_signal(ready.at[0], inc=1, device_id=x_up, device_id_type=MESH)
+    pl.semaphore_signal(ready.at[1], inc=1, device_id=(me, (y + 1) % NY), device_id_type=MESH)
 
     def remote(src, dst, send, recv, device):
         return pltpu.make_async_remote_copy(
@@ -92,14 +107,12 @@
     ]
     for swap in swaps:
         swap.start()
-    halos = []
-    for back in (1, 2):
-        rows = pl.ds(pl.multiple_of((2 - back) * 2 * TOK + core * TOK, TOK), TOK)
-        for head in range(2):
-            halos.append(remote(
-                span_heads.at[head], window.at[rows, :],
-                halo_send.at[back - 1, head], halo_recv.at[back - 1, core],
-                linear(back, head)))
+    halos = [
+        remote(window.at[2 * FAR:3 * FAR, :], window.at[FAR:2 * FAR, :],
+               halo_send.at[0], halo_recv.at[0], after),
+        remote(window.at[FAR + BLK:2 * FAR, :], window.at[BLK:FAR, :],
+               halo_send.at[1], halo_recv.at[1], after),
+    ]
 
     def row_of(k):
         return (z + NZ + (1 - 2 * (k % 2)) * ((k + 1) // 2)) % NZ
@@ -110,16 +123,18 @@
                       piece_recv.at[k_there, off_there], device)
 
     def along_z(k, off, act):
+        last_up, last_down = (3, 6) if off == 0 else (1, 4)
+
         @pl.when(k == 0)
         def _():
             act(piece(k, off, 0, z_up, 1, off))
             act(piece(k, off, 1, z_down, 2, off))
 
-        @pl.when((k % 2 == 1) & (k <= 3))
+        @pl.when((k % 2 == 1) & (k <= last_up))
         def _():
             act(piece(k, off, 0, z_up, k + 2, off))
 
-        @pl.when((k % 2 == 0) & (k >= 2))
+        @pl.when((k % 2 == 0) & (k >= 2) & (k <= last_down))
         def _():
             act(piece(k, off, 1, z_down, k + 2 - k // 6, off))
 
@@ -131,14 +146,23 @@
         def _():
             act(piece(k, 0, 4, x_far, k, 2))
 
+    def relays_up(k):
+        return (k % 2 == 1) & (k < 7)
+
+    def relays_down(k):
+        return ((k % 2 == 0) & (k >= 2)) | (k == 7)
+
     def relay_x(k, act):
-        @pl.when(k % 2 == 1)
+        @pl.when(relays_up(k))
         def _():
             act(piece(k, 3, 2, x_up, k, 2))
 
-        @pl.when((k % 2 == 0) & (k >= 2))
+        @pl.when(relays_down(k))
         def _():
             act(piece(k, 1, 3, x_down, k, 2))
+
+    def column_first(k):
+        return (core == 1) | (k == 5) | (k == 7)
 
     def begin(copy):
         copy.start()
@@ -153,23 +177,47 @@
     def stage_a(k):
         arrive(k, 0)
         along_z(k, 0, begin)
-        along_x(k, begin)
+
+        @pl.when(column_first(k))
+        def _():
+            along_x(k, begin)
 
     def stage_b(k):
-        @pl.when(k % 2 == 1)
-        def _():
-            arrive(k, 3)
-
-        @pl.when(k % 2 == 0)
-        def _():
-            arrive(k, 1)
-        relay_x(k, begin)
+        @pl.when(column_first(k))
+        def _():
+            @pl.when(relays_up(k))
+            def _():
+                arrive(k, 3)
+
+            @pl.when(relays_down(k))
+            def _():
+                arrive(k, 1)
+            relay_x(k, begin)
+
+    def stage_c(k):
+        @pl.when(column_first(k))
+        def _():
+            @pl.when((k == 0) | relays_up(k))
+            def _():
+                arrive(k, 1)
+
+            @pl.when((k == 0) | relays_down(k))
+            def _():
+                arrive(k, 3)
+            arrive(k, 2)
+
+        @pl.when(jnp.logical_not(column_first(k)))
+        def _():
+            for off in (1, 3, 2):
+                arrive(k, off)
+                along_z(k, off, begin)
 
     swaps[0].wait_recv()
+    pl.semaphore_wait(ready.at[0], 1)
     along_z(0, 0, begin)
     along_x(0, begin)
-    for halo in halos:
-        halo.start()
+    swaps[2].wait_recv()
+    halos[0].start()
 
     load_q.wait()
     swaps[1].wait_recv()
@@ -209,15 +257,13 @@
             preferred_element_type=jnp.float32)
 
     def slash():
-        for back in (1, 2):
-            for which in range(2):
-                rows = window.at[(2 - back) * 2 * TOK + which * TOK:(2 - back) * 2 * TOK + (which + 1) * TOK, :]
-                remote(rows, rows, halo_send.at[back - 1, 0], halo_recv.at[back - 1, which], partner).wait_recv()
-        swaps[2].wait_recv()
-        wk[:, 0:HD] = window[:, 0:HD]
-        lane = lax.broadcasted_iota(jnp.int32, (WINDOW, HD), 1)
-        wk[:, HD:2 * HD] = jnp.where(lane == HD - 1, jnp.zeros((WINDOW, HD), jnp.bfloat16), window[:, 0:HD])
-        wv[:, 0:HD] = window[:, HD:2 * HD]
+        halos[1].wait_recv()
+        rows = slice(BLK, WINDOW)
+        wk[rows, 0:HD] = window[rows, 0:HD]
+        lane = lax.broadcasted_iota(jnp.int32, (WINDOW - BLK, HD), 1)
+        wk[rows, HD:2 * HD] = jnp.where(
+            lane == HD - 1, jnp.zeros((WINDOW - BLK, HD), jnp.bfloat16), window[rows, 0:HD])
+        wv[rows, 0:HD] = window[rows, HD:2 * HD]
         for n in range(CHUNKS):
             place = core if n < NY else other
             first = ((y + n % NY) % NY) * SUB
@@ -229,68 +275,50 @@
             scores = jnp.where(allowed, score(n, wk[keys, :]), FLOOR)
             update(n, scores, wv[keys, :])
 
-    def tile(k):
+    def load_tile(k):
         row = row_of(k)
         lane = lax.broadcasted_iota(jnp.int32, (BLK, HD), 1)
         for cx in range(NX):
             for b in range(4):
                 owner = 2 * (cx * NZ + row) + b // 2
-                fill = jnp.full((BLK, HD), bias[core, 2 * owner + b % 2], jnp.float32)
+                fill = jnp.broadcast_to(bias[b % 2, pl.ds(owner, 1), :], (BLK, HD))
                 rows = slice(b * BLK, (b + 1) * BLK)
                 there = slice(cx * CHUNK_KEYS + b * BLK, cx * CHUNK_KEYS + (b + 1) * BLK)
                 keys = gathered[row, cx, rows, 0:HD]
                 k2[there, 0:HD] = keys
                 k2[there, HD:2 * HD] = jnp.where(lane == HD - 1, fill.astype(jnp.bfloat16), keys)
                 v2[there, 0:HD] = gathered[row, cx, rows, HD:2 * HD]
+
+    stage_a(1)
+    halos[0].wait_recv()
+    halos[1].start()
+
+    def step(k, carry):
+        @pl.when(k + 2 < NZ)
+        def _():
+            stage_a(k + 2)
+
+        stage_b(k + 1)
+        stage_c(k)
+        load_tile(k)
         for n in range(CHUNKS):
             update(n, score(n, k2[...]), v2[...])
 
-    @pl.when(core == 1)
-    def _():
-        stage_a(1)
-
-    def step(k, carry):
-        @pl.when(core == 0)
-        def _():
-            @pl.when(k > 0)
-            def _():
-                arrive(k, 0)
-                along_z(k, 0, begin)
-            for off in (1, 3, 2):
-                arrive(k, off)
-                along_z(k, off, begin)
-
-        @pl.when(core == 1)
-        def _():
-            @pl.when(k + 2 < NZ)
-            def _():
-                stage_a(k + 2)
-
-            @pl.when(k + 1 < NZ)
-            def _():
-                stage_b(k + 1)
-
-            @pl.when((k == 0) | (k % 2 == 1))
-            def _():
-                arrive(k, 1)
-
-            @pl.when(k % 2 == 0)
-            def _():
-                arrive(k, 3)
-            arrive(k, 2)
-        tile(k)
-
         @pl.when(k == 0)
         def _():
             slash()
         return carry
 
-    lax.fori_loop(0, NZ, step, 0)
+    lax.fori_loop(0, NZ - 1, step, 0)
+    stage_c(NZ - 1)
+    load_tile(NZ - 1)
+    pl.semaphore_wait(ready.at[1], 1)
 
     out_columns = pl.ds(pl.multiple_of(y * 2 * QW + core * QW, QW), QW)
     sends = []
     keep_own = pltpu.make_async_copy(slab.at[0], out_hbm.at[:, out_columns], own_sem)
     for n in (2, 6, 1, 5, 3, 7, 4, 0):
+        update(n, score(n, k2[...]), v2[...])
         rows = slice(n * ROWS, (n + 1) * ROWS)
         done = (acc[rows, 0:HD] / acc[rows, HD:2 * HD]).astype(jnp.bfloat16)
         for h in range(GROUP):
@@ -312,19 +340,18 @@
     def finish(k, carry):
         along_z(k, 0, drain)
 
-        @pl.when(core == 0)
+        @pl.when((k == 0) | column_first(k))
+        def _():
+            along_x(k, drain)
+
+        @pl.when(column_first(k))
+        def _():
+            relay_x(k, drain)
+
+        @pl.when(jnp.logical_not(column_first(k)))
         def _():
             for off in (1, 2, 3):
                 along_z(k, off, drain)
-
-            @pl.when(k == 0)
-            def _():
-                along_x(k, drain)
-
-        @pl.when(core == 1)
-        def _():
-            along_x(k, drain)
-            relay_x(k, drain)
         return carry
 
     lax.fori_loop(0, NZ, finish, 0)
@@ -334,32 +361,18 @@
 
 
 def body(queries, span_kv, cache_kv, verticals, offsets):
-    heads = span_kv.shape[1]
-    owners = lax.axis_size("ctx")
-    my_index = lax.axis_index("ctx")
     cache_blocks = cache_kv.shape[0] // BLK
-    owner_of = verticals // cache_blocks
-    in_owner = verticals % cache_blocks
-    is_mine = owner_of == my_index
-    rank = jnp.cumsum(is_mine.astype(jnp.int32), axis=1) - 1
-    slots = jnp.arange(2, dtype=jnp.int32)
-    hit = is_mine[:, None, :] & (rank[:, None, :] == slots[None, :, None])
-    picks = jnp.sum(jnp.where(hit, in_owner[:, None, :], 0), axis=2)
-    held = jnp.sum(
-        (owner_of[:, None, :] == jnp.arange(owners, dtype=jnp.int32)[None, :, None]).astype(jnp.int32),
-        axis=2)
-    bias = jnp.where(slots[None, None, :] < held[:, :, None], 0.0, DEAD).astype(jnp.float32)
-    bias = bias.reshape(heads, 2 * owners)
     bf16 = jnp.bfloat16
     any_space = pl.BlockSpec(memory_space=pl.ANY)
-    smem = pl.BlockSpec(memory_space=pltpu.SMEM)
     dma = pltpu.SemaphoreType.DMA
     return pl.pallas_call(
         kernel,
         out_shape=jax.ShapeDtypeStruct((SUB, 4 * 2 * QW), bf16),
-        in_specs=[smem, smem, any_space, any_space, any_space],
+        in_specs=[any_space] * 4,
         out_specs=any_space,
         scratch_shapes=[
+            pltpu.VMEM((2, NV), jnp.int32),
+            pltpu.VMEM((2, 2 * CHIPS, HD), jnp.float32),
             pltpu.VMEM((cache_blocks, BLK) + cache_kv.shape[1:], bf16),
             pltpu.VMEM(span_kv.shape, bf16),
             pltpu.VMEM((2, TOK, 2 * HD), bf16),
@@ -376,12 +389,12 @@
             pltpu.VMEM((CHUNKS * ROWS, 2 * HD), jnp.float32),
             pltpu.VMEM((CHUNKS * ROWS, HD), jnp.float32),
             pltpu.VMEM((CHUNKS, SUB, QW), bf16),
-            dma((3,)), dma((3,)), dma((3,)), dma((2, 2)), dma((2, 2)),
+            dma((4,)), dma((3,)), dma((3,)), dma((2,)), dma((2,)), pltpu.SemaphoreType.REGULAR((2,)),
             dma((NZ, NX, 5)), dma((NZ, NX)), dma((CHUNKS,)), dma((CHUNKS,)), dma,
         ],
         compiler_params=pltpu.CompilerParams(
             collective_id=0, has_side_effects=True, vmem_limit_bytes=60 << 20),
-    )(picks, bias, queries, span_kv, cache_kv.reshape((cache_blocks, BLK) + cache_kv.shape[1:]))
+    )(verticals, queries, span_kv, cache_kv.reshape((cache_blocks, BLK) + cache_kv.shape[1:]))
 
 
 def solution(mesh):

time: 76.8 us -> 69.1 us (0.90)
  Pallas kernels: 71.3 us -> 67.1 us
  other arithmetic: 3.05 us -> 0 us
    pallas_call x1, Pallas kernels: 71.3 us -> 67.1 us  [body(): pl.pallas_call(kernel, out_shape=jax.ShapeDtypeStruct((SUB, 4 * 2 * QW),...]
    select_n x2 -> x0, other arithmetic: 1.3 us -> none  [the longest x1 0.69 us: body(): in_owner = verticals % cache_blocks]
    reduce_sum x2 -> x0, other arithmetic: 0.82 us -> none  [the longest x1 0.71 us: body(): picks = jnp.sum(jnp.where(hit, in_owner[:, None, :], 0), axis=2)]
where the time goes in v2:
time: 69.1 us; the launch traced here: 68.9 us
  Pallas kernels  67.1 us (97%)
  local copies, waits for them, and re-layouts  1.87 us (3%)
    pallas_call x1, Pallas kernels, body(): pl.pallas_call(kernel, out_shape=jax.ShapeDtypeStruct((SUB, 4 * 2 * QW),...  67.1 us
    unnamed x1, local copies, waits for them, and re-layouts  1.87 us

profile of v2, /device:TPU:1, one launch (start us, length us, event | category | flops | bytes accessed | tf_op | source)
XLA Modules:
  0.0 68.9 jit_solution(2813405924908726413)
XLA Ops:
  0.0 67.1 %shard_map.46 = bf16[32,8192]{1,0:T(8,128)(2,1)} custom-call(s32[2,64]{1,0:T(2,128)} %verts_hbm.1, bf16[128,2048]{1,0:T(8,128)(2,1)} %q_hbm.1, bf16[128,2,256]{2,1,0:T(2,128)(2,1)} %span_hbm.1, bf16[64,64,2,256]{3,2,1,0:T(2,128)(2,1)} %bitcast.1), custom_call_target="tpu_custom_call" | custom-call | tf_op jit(solution)/shard_map/pallas_call | solution.py:368
  67.1 1.9 %copy.6 = bf16[32,8192]{1,0:T(8,128)(2,1)} copy(bf16[32,8192]{1,0:T(8,128)(2,1)} %shard_map.46) | data formatting | bytes 1048576

commit v3 on v2

--- a/solution.py
+++ b/solution.py
@@ -19,6 +19,7 @@
 FAR = 2 * TOK
 WINDOW = 3 * FAR
 NV = 64
+HALO_AT, RELAY_AT = 0, 2
 QW = GROUP * HD
 FLOOR = -1e30
 DEAD = -30000.0
@@ -216,8 +217,6 @@
     pl.semaphore_wait(ready.at[0], 1)
     along_z(0, 0, begin)
     along_x(0, begin)
-    swaps[2].wait_recv()
-    halos[0].start()
 
     load_q.wait()
     swaps[1].wait_recv()
@@ -256,7 +255,7 @@
             q2[n * ROWS:(n + 1) * ROWS, :], keys, (((1,), (1,)), ((), ())),
             preferred_element_type=jnp.float32)
 
-    def slash():
+    def load_window():
         halos[1].wait_recv()
         rows = slice(BLK, WINDOW)
         wk[rows, 0:HD] = window[rows, 0:HD]
@@ -264,16 +263,17 @@
         wk[rows, HD:2 * HD] = jnp.where(
             lane == HD - 1, jnp.zeros((WINDOW - BLK, HD), jnp.bfloat16), window[rows, 0:HD])
         wv[rows, 0:HD] = window[rows, HD:2 * HD]
-        for n in range(CHUNKS):
-            place = core if n < NY else other
-            first = ((y + n % NY) % NY) * SUB
-            block = 2 * place + first // BLK
-            keys = pl.ds(pl.multiple_of((block + 1) * BLK, BLK), 8 * BLK)
-            column = lax.broadcasted_iota(jnp.int32, (ROWS, 8 * BLK), 1)
-            token = lax.broadcasted_iota(jnp.int32, (ROWS, 8 * BLK), 0) % SUB + first % BLK
-            allowed = (column <= 7 * BLK + token) & (column >= (7 - block - 4 * chip) * BLK)
-            scores = jnp.where(allowed, score(n, wk[keys, :]), FLOOR)
-            update(n, scores, wv[keys, :])
+
+    def slash(n):
+        place = core if n < NY else other
+        first = ((y + n % NY) % NY) * SUB
+        block = 2 * place + first // BLK
+        keys = pl.ds(pl.multiple_of((block + 1) * BLK, BLK), 8 * BLK)
+        column = lax.broadcasted_iota(jnp.int32, (ROWS, 8 * BLK), 1)
+        token = lax.broadcasted_iota(jnp.int32, (ROWS, 8 * BLK), 0) % SUB + first % BLK
+        allowed = (column <= 7 * BLK + token) & (column >= (7 - block - 4 * chip) * BLK)
+        scores = jnp.where(allowed, score(n, wk[keys, :]), FLOOR)
+        update(n, scores, wv[keys, :])
 
     def load_tile(k):
         row = row_of(k)
@@ -290,8 +290,6 @@
                 v2[there, 0:HD] = gathered[row, cx, rows, HD:2 * HD]
 
     stage_a(1)
-    halos[0].wait_recv()
-    halos[1].start()
 
     def step(k, carry):
         @pl.when(k + 2 < NZ)
@@ -300,18 +298,25 @@
 
         stage_b(k + 1)
         stage_c(k)
+
+        @pl.when(k == HALO_AT)
+        def _():
+            swaps[2].wait_recv()
+            halos[0].start()
+
+        @pl.when(k == RELAY_AT)
+        def _():
+            halos[0].wait_recv()
+            halos[1].start()
         load_tile(k)
         for n in range(CHUNKS):
             update(n, score(n, k2[...]), v2[...])
-
-        @pl.when(k == 0)
-        def _():
-            slash()
         return carry
 
     lax.fori_loop(0, NZ - 1, step, 0)
     stage_c(NZ - 1)
     load_tile(NZ - 1)
+    load_window()
     pl.semaphore_wait(ready.at[1], 1)
 
     out_columns = pl.ds(pl.multiple_of(y * 2 * QW + core * QW, QW), QW)
@@ -319,6 +324,7 @@
     keep_own = pltpu.make_async_copy(slab.at[0], out_hbm.at[:, out_columns], own_sem)
     for n in (2, 6, 1, 5, 3, 7, 4, 0):
         update(n, score(n, k2[...]), v2[...])
+        slash(n)
         rows = slice(n * ROWS, (n + 1) * ROWS)
         done = (acc[rows, 0:HD] / acc[rows, HD:2 * HD]).astype(jnp.bfloat16)
         for h in range(GROUP):

time: 69.1 us -> 67.1 us (0.971)
  Pallas kernels: 67.1 us -> 65.1 us
    pallas_call x1, Pallas kernels: 67.1 us -> 65.1 us  [body(): pl.pallas_call(kernel, out_shape=jax.ShapeDtypeStruct((SUB, 4 * 2 * QW),...]
where the time goes in v3:
time: 67.1 us; the launch traced here: 67 us
  Pallas kernels  65.1 us (97%)
  local copies, waits for them, and re-layouts  1.87 us (3%)
    pallas_call x1, Pallas kernels, body(): pl.pallas_call(kernel, out_shape=jax.ShapeDtypeStruct((SUB, 4 * 2 * QW),...  65.1 us
    unnamed x1, local copies, waits for them, and re-layouts  1.87 us

profile of v3, /device:TPU:1, one launch (start us, length us, event | category | flops | bytes accessed | tf_op | source)
XLA Modules:
  0.0 67.0 jit_solution(10792235424093755763)
XLA Ops:
  0.0 65.1 %shard_map.46 = bf16[32,8192]{1,0:T(8,128)(2,1)} custom-call(s32[2,64]{1,0:T(2,128)} %verts_hbm.1, bf16[128,2048]{1,0:T(8,128)(2,1)} %q_hbm.1, bf16[128,2,256]{2,1,0:T(2,128)(2,1)} %span_hbm.1, bf16[64,64,2,256]{3,2,1,0:T(2,128)(2,1)} %bitcast.1), custom_call_target="tpu_custom_call" | custom-call | tf_op jit(solution)/shard_map/pallas_call | solution.py:374
  65.1 1.9 %copy.6 = bf16[32,8192]{1,0:T(8,128)(2,1)} copy(bf16[32,8192]{1,0:T(8,128)(2,1)} %shard_map.46) | data formatting | bytes 1048576

commit v4 on v3

--- a/solution.py
+++ b/solution.py
@@ -143,7 +143,7 @@
         act(piece(k, 0, 2, x_up, k, 3))
         act(piece(k, 0, 3, x_down, k, 1))
 
-        @pl.when(k == 0)
+        @pl.when((k == 0) & (core == 0))
         def _():
             act(piece(k, 0, 4, x_far, k, 2))
 
@@ -151,7 +151,7 @@
         return (k % 2 == 1) & (k < 7)
 
     def relays_down(k):
-        return ((k % 2 == 0) & (k >= 2)) | (k == 7)
+        return (k % 2 == 0) | (k == 7)
 
     def relay_x(k, act):
         @pl.when(relays_up(k))
@@ -198,11 +198,11 @@
     def stage_c(k):
         @pl.when(column_first(k))
         def _():
-            @pl.when((k == 0) | relays_up(k))
+            @pl.when(relays_up(k))
             def _():
                 arrive(k, 1)
 
-            @pl.when((k == 0) | relays_down(k))
+            @pl.when(relays_down(k))
             def _():
                 arrive(k, 3)
             arrive(k, 2)
@@ -290,6 +290,7 @@
                 v2[there, 0:HD] = gathered[row, cx, rows, HD:2 * HD]
 
     stage_a(1)
+    stage_b(0)
 
     def step(k, carry):
         @pl.when(k + 2 < NZ)

time: 67.1 us -> 66 us (0.984)
  Pallas kernels: 65.1 us -> 64 us
    pallas_call x1, Pallas kernels: 65.1 us -> 64 us  [body(): pl.pallas_call(kernel, out_shape=jax.ShapeDtypeStruct((SUB, 4 * 2 * QW),...]
where the time goes in v4:
time: 66 us; the launch traced here: 65.8 us
  Pallas kernels  64 us (97%)
  local copies, waits for them, and re-layouts  1.87 us (3%)
    pallas_call x1, Pallas kernels, body(): pl.pallas_call(kernel, out_shape=jax.ShapeDtypeStruct((SUB, 4 * 2 * QW),...  64 us
    unnamed x1, local copies, waits for them, and re-layouts  1.87 us

profile of v4, /device:TPU:1, one launch (start us, length us, event | category | flops | bytes accessed | tf_op | source)
XLA Modules:
  0.0 65.8 jit_solution(14167568756150383058)
XLA Ops:
  0.0 64.0 %shard_map.46 = bf16[32,8192]{1,0:T(8,128)(2,1)} custom-call(s32[2,64]{1,0:T(2,128)} %verts_hbm.1, bf16[128,2048]{1,0:T(8,128)(2,1)} %q_hbm.1, bf16[128,2,256]{2,1,0:T(2,128)(2,1)} %span_hbm.1, bf16[64,64,2,256]{3,2,1,0:T(2,128)(2,1)} %bitcast.1), custom_call_target="tpu_custom_call" | custom-call | tf_op jit(solution)/shard_map/pallas_call | solution.py:375
  64.0 1.9 %copy.6 = bf16[32,8192]{1,0:T(8,128)(2,1)} copy(bf16[32,8192]{1,0:T(8,128)(2,1)} %shard_map.46) | data formatting | bytes 1048576

commit v5 on v4

--- a/solution.py
+++ b/solution.py
@@ -19,7 +19,7 @@
 FAR = 2 * TOK
 WINDOW = 3 * FAR
 NV = 64
-HALO_AT, RELAY_AT = 0, 2
+HALO_AT, RELAY_AT = 1, 3
 QW = GROUP * HD
 FLOOR = -1e30
 DEAD = -30000.0

time: 66 us -> 66.7 us (1.011)
  Pallas kernels: 64 us -> 64.7 us
    pallas_call x1, Pallas kernels: 64 us -> 64.7 us  [body(): pl.pallas_call(kernel, out_shape=jax.ShapeDtypeStruct((SUB, 4 * 2 * QW),...]
where the time goes in v5:
time: 66.7 us; the launch traced here: 66.6 us
  Pallas kernels  64.7 us (97%)
  local copies, waits for them, and re-layouts  1.87 us (3%)
    pallas_call x1, Pallas kernels, body(): pl.pallas_call(kernel, out_shape=jax.ShapeDtypeStruct((SUB, 4 * 2 * QW),...  64.7 us
    unnamed x1, local copies, waits for them, and re-layouts  1.87 us

profile of v5, /device:TPU:1, one launch (start us, length us, event | category | flops | bytes accessed | tf_op | source)
XLA Modules:
  0.0 66.6 jit_solution(163620360131310427)
XLA Ops:
  0.0 64.7 %shard_map.46 = bf16[32,8192]{1,0:T(8,128)(2,1)} custom-call(s32[2,64]{1,0:T(2,128)} %verts_hbm.1, bf16[128,2048]{1,0:T(8,128)(2,1)} %q_hbm.1, bf16[128,2,256]{2,1,0:T(2,128)(2,1)} %span_hbm.1, bf16[64,64,2,256]{3,2,1,0:T(2,128)(2,1)} %bitcast.1), custom_call_target="tpu_custom_call" | custom-call | tf_op jit(solution)/shard_map/pallas_call | solution.py:375
  64.7 1.9 %copy.6 = bf16[32,8192]{1,0:T(8,128)(2,1)} copy(bf16[32,8192]{1,0:T(8,128)(2,1)} %shard_map.46) | data formatting | bytes 1048576
